TPU v7x, 32 devices: a whole 2x2x4 slice. The times are simulated.
32 devices in a mesh: tm: 16 (over z, y, x), rows: 2 (over core).
Axes of the slice: x: 2, y: 2, z: 4, core: 2. Of those that a mesh axis runs over, the one named last changes fastest.
Arguments:
- latents: bfloat16 [64, 8, 5120], P('tm', 'rows'), may hold values from -25 to 25
- cotangent: bfloat16 [64, 8, 5120], P('tm', 'rows'), may hold values from -6 to 6
- kernel_one: bfloat16 [3, 3, 3, 64, 64], replicated, may hold values from -0.15625 to 0.15625
- kernel_two: bfloat16 [3, 3, 3, 64, 64], replicated, may hold values from -0.15625 to 0.15625
- gain_one: float32 [64], replicated, may hold values from 0.5 to 1.5
- offset_one: float32 [64], replicated, may hold values from -3 to 3
- gain_two: float32 [64], replicated, may hold values from 0.5 to 1.5
- offset_two: float32 [64], replicated, may hold values from -3 to 3
- clip_id: int32 [64], P('tm'), may hold values from 0 to 7, never falling along the last dimension, each value on 1 to 16 neighbouring positions
Outputs:
- output: bfloat16 [64, 8, 5120], P('tm', 'rows')
- grad_latent: bfloat16 [64, 8, 5120], P('tm', 'rows')
- grad_kernel_one: float32 [3, 3, 3, 64, 64], replicated
- grad_kernel_two: float32 [3, 3, 3, 64, 64], replicated
Inputs may be any that keep to these rules, and one draw needn't show every extreme that they name: `clip_id`: clip numbers never fall along the frames; each clip number 0 to 7 names 1 to 16 consecutive frames, and one clip has exactly 16.
All inputs are finite; a program needn't handle non-finite values.
Results may differ from a plain program's by a relative error of at most 0.0085.
Values may be sent and summed in bfloat16 or wider, within the bound.
A program may use at most 128 MiB of HBM per device.

v0:
```python
import jax
import jax.numpy as jnp
from jax import lax
from jax.sharding import PartitionSpec as P

GROUPS = 32
EPSILON = 1e-06
HIGHEST = lax.Precision.HIGHEST


def with_halo(block, sides, width):
    for axis, dim in sides:
        count = lax.axis_size(axis)
        forward = [(i, i + 1) for i in range(count - 1)]
        backward = [(target, source) for source, target in forward]
        low = lax.ppermute(
            lax.slice_in_dim(block, block.shape[dim] - width, None, axis=dim), axis, forward
        )
        high = lax.ppermute(lax.slice_in_dim(block, 0, width, axis=dim), axis, backward)
        block = jnp.concatenate([low, block, high], axis=dim)
    return block


def passed_along(value, axis, by):
    length = lax.axis_size(axis)
    pairs = [(i, i + by) for i in range(length) if 0 <= i + by < length]
    return lax.ppermute(value, axis, pairs)


def row_halo(extended):
    return with_halo(extended, (("rows", 1),), 1)


def spread(extended, channels):
    depth, height, flat = extended.shape
    shaped = extended.reshape(depth, height, flat // channels, channels)
    return jnp.pad(shaped, ((0, 0), (0, 0), (1, 1), (0, 0)))


def forward_taps(frames, n_rows, n_cols):
    taps = [
        frames[:, row_tap : row_tap + n_rows, col_tap : col_tap + n_cols]
        for row_tap in range(3)
        for col_tap in range(3)
    ]
    joined = jnp.concatenate(taps, axis=-1)
    return joined.reshape(-1, joined.shape[-1])


def reverse_taps(frames, n_rows, n_cols):
    taps = [
        frames[:, 2 - row_tap : 2 - row_tap + n_rows, 2 - col_tap : 2 - col_tap + n_cols]
        for row_tap in range(3)
        for col_tap in range(3)
    ]
    joined = jnp.concatenate(taps, axis=-1)
    return joined.reshape(-1, joined.shape[-1])


def causal_conv(field, tags, kernel):
    n_frames, n_rows, flat = field.shape
    channels = kernel.shape[3]
    n_cols = flat // channels
    past_field, past_tags = passed_along((field[-2:], tags[-2:]), "tm", 1)
    padded = spread(row_halo(jnp.concatenate([past_field, field], axis=0)), channels)
    all_tags = jnp.concatenate([past_tags, tags])
    result = jnp.zeros((n_frames * n_rows * n_cols, kernel.shape[4]), jnp.float32)
    patch_list = []
    for lag in range(3):
        lag_mask = (all_tags[2 - lag : 2 - lag + n_frames] == tags).astype(jnp.bfloat16)
        frames = padded[2 - lag : 2 - lag + n_frames] * lag_mask[:, None, None, None]
        patches = forward_taps(frames, n_rows, n_cols)
        patch_list.append(patches)
        result = result + jnp.dot(
            patches, kernel[lag].reshape(-1, kernel.shape[4]), preferred_element_type=jnp.float32
        )
    return (result.reshape(n_frames, n_rows, flat), patch_list)


def transposed_conv(grad, tags, kernel):
    n_frames, n_rows, flat = grad.shape
    channels = kernel.shape[3]
    n_cols = flat // channels
    next_grad, next_tags = passed_along((grad[:2], tags[:2]), "tm", -1)
    padded = spread(row_halo(jnp.concatenate([grad, next_grad], axis=0)), channels)
    all_tags = jnp.concatenate([tags, next_tags])
    result = jnp.zeros((n_frames * n_rows * n_cols, channels), jnp.float32)
    for lag in range(3):
        lag_mask = (all_tags[lag : lag + n_frames] == tags).astype(jnp.bfloat16)
        frames = padded[lag : lag + n_frames] * lag_mask[:, None, None, None]
        patches = reverse_taps(frames, n_rows, n_cols)
        flipped = jnp.swapaxes(kernel[lag], 2, 3).reshape(-1, channels)
        result = result + jnp.dot(patches, flipped, preferred_element_type=jnp.float32)
    return result.reshape(n_frames, n_rows, flat)


def kernel_grad(patch_list, grad, channels):
    flat_grad = grad.reshape(-1, channels)
    stacked = [
        lax.dot_general(
            patches, flat_grad, (((0,), (0,)), ((), ())), preferred_element_type=jnp.float32
        ).reshape(3, 3, channels, channels)
        for patches in patch_list
    ]
    return jnp.stack(stacked)


def clip_totals(first, second, ones_col, clip_id):
    clips = lax.axis_size("tm") // 2
    onehot = (clip_id[:, None] == jnp.arange(clips, dtype=jnp.int32)[None, :]).astype(jnp.float32)
    table_a = jnp.dot(onehot.T, first, precision=HIGHEST)
    table_b = jnp.dot(onehot.T, second, precision=HIGHEST)
    table_c = jnp.dot(onehot.T, ones_col, precision=HIGHEST)
    summed_a, summed_b, summed_c = lax.psum((table_a, table_b, table_c), ("tm", "rows"))
    return (
        jnp.dot(onehot, summed_a, precision=HIGHEST),
        jnp.dot(onehot, summed_b, precision=HIGHEST),
        jnp.dot(onehot, summed_c, precision=HIGHEST),
    )


def norm_forward(field, gain, offset, clip_id):
    n_frames, n_rows, flat = field.shape
    channels = gain.shape[0]
    per_group = channels // GROUPS
    grouped = field.reshape(n_frames, n_rows * (flat // channels), GROUPS, per_group)
    first = jnp.sum(grouped, axis=(1, 3))
    second = jnp.sum(grouped * grouped, axis=(1, 3))
    ones_col = jnp.ones((n_frames, 1), jnp.float32)
    total_a, total_b, total_c = clip_totals(first, second, ones_col, clip_id)
    cells_count = total_c * float(grouped.shape[1] * per_group)
    mean_val = total_a / cells_count
    square_mean = total_b / cells_count
    inv_std = lax.rsqrt(square_mean - mean_val * mean_val + EPSILON)
    normed = (grouped - mean_val[:, None, :, None]) * inv_std[:, None, :, None]
    z_value = normed * gain.reshape(1, 1, GROUPS, per_group) + offset.reshape(
        1, 1, GROUPS, per_group
    )
    return (normed, z_value, inv_std, cells_count)


def norm_backward(grad, normed, z_value, inv_std, cells_count, gain, clip_id):
    per_group = normed.shape[3]
    grouped_grad = grad.reshape(normed.shape)
    sigmoid_z = jax.nn.sigmoid(z_value)
    grad_norm = (
        grouped_grad
        * sigmoid_z
        * (1.0 + z_value * (1.0 - sigmoid_z))
        * gain.reshape(1, 1, GROUPS, per_group)
    )
    first = jnp.sum(grad_norm, axis=(1, 3))
    second = jnp.sum(grad_norm * normed, axis=(1, 3))
    ones_col = jnp.ones((normed.shape[0], 1), jnp.float32)
    total_a, total_b, total_c = clip_totals(first, second, ones_col, clip_id)
    p_term = total_a / cells_count
    q_term = total_b / cells_count
    result = inv_std[:, None, :, None] * (
        grad_norm - p_term[:, None, :, None] - normed * q_term[:, None, :, None]
    )
    return result.reshape(grad.shape)


def per_device(
    latents, cotangent, kernel_one, kernel_two, gain_one, offset_one, gain_two, offset_two, clip_id
):
    channels = gain_one.shape[0]
    tags = (clip_id + 1).astype(jnp.bfloat16)
    field = latents.astype(jnp.float32)
    normed_one, z_one, inv_one, cells_count = norm_forward(field, gain_one, offset_one, clip_id)
    act_one = jax.nn.silu(z_one).astype(jnp.bfloat16).reshape(latents.shape)
    conv_one, patches_one = causal_conv(act_one, tags, kernel_one)
    hidden = conv_one.astype(jnp.bfloat16)
    normed_two, z_two, inv_two, count_again = norm_forward(
        hidden.astype(jnp.float32), gain_two, offset_two, clip_id
    )
    act_two = jax.nn.silu(z_two).astype(jnp.bfloat16).reshape(latents.shape)
    conv_two, patches_two = causal_conv(act_two, tags, kernel_two)
    output = (field + conv_two).astype(jnp.bfloat16)
    grad_two = kernel_grad(patches_two, cotangent, channels)
    back_two = transposed_conv(cotangent, tags, kernel_two)
    grad_hidden = norm_backward(
        back_two, normed_two, z_two, inv_two, count_again, gain_two, clip_id
    ).astype(jnp.bfloat16)
    grad_one = kernel_grad(patches_one, grad_hidden, channels)
    back_one = transposed_conv(grad_hidden, tags, kernel_one)
    branch = norm_backward(back_one, normed_one, z_one, inv_one, cells_count, gain_one, clip_id)
    grad_latent = (cotangent.astype(jnp.float32) + branch).astype(jnp.bfloat16)
    grad_one, grad_two = lax.psum((grad_one, grad_two), ("tm", "rows"))
    return (output, grad_latent, grad_one, grad_two)


def solution(mesh):
    return jax.shard_map(
        per_device,
        mesh=mesh,
        in_specs=(
            P("tm", "rows", None),
            P("tm", "rows", None),
            P(),
            P(),
            P(),
            P(),
            P(),
            P(),
            P("tm"),
        ),
        out_specs=(P("tm", "rows", None), P("tm", "rows", None), P(), P()),
        check_vma=False,
    )
```

profile of v0, /device:TPU:0, one launch (start us, length us, event | category | flops | bytes accessed | tf_op | source)
XLA Modules:
  0.0 727.7 jit_solution(2860579713837529750)
XLA Ops:
  9.2 5.5 collective-permute-start.3
  17.8 5.6 copy.294
  23.4 11.2 %fusion.74 = (f32[4,32]{0,1:T(8,128)S(1)}, f32[4,32]{0,1:T(8,128)S(1)}) fusion(f32[4,320,32,2]{0,3,2,1:T(2,128)} %bitcast.178), kind=kLoop, calls=%fused_computation.168 | loop fusion | flops 245504 | bytes 328704 | tf_op jit(solution)/shard_map/reduce_sum | solution.py:127
  34.7 10.2 %copy.295 = f32[4,320,32,2]{1,2,3,0:T(8,128)S(1)} copy(f32[4,320,32,2]{0,3,2,1:T(2,128)} %bitcast.179) | data formatting | bytes 655360 | tf_op jit(solution)/shard_map/reshape | solution.py:126
  45.8 45.0 %all-reduce.7 = (f32[8,32]{1,0:T(8,128)S(1)}, f32[8,32]{1,0:T(8,128)S(1)}, f32[8]{0:T(128)S(1)}) all-reduce(f32[8,32]{1,0:T(8,128)S(1)} %fusion.49, f32[8,32]{1,0:T(8,128)S(1)} %fusion.51, f32[8]{0:T(128)S(1)} %convolution_bitcast_fusion.7), channel_id=1, replica_groups=mesh['tm'=16,'rows'=2] {'tm','rows'}, use_global_device_ids=true, to_apply=%region_4.0 | all-reduce | flops 520 | bytes 4160 | tf_op jit(solution)/shard_map/psum | solution.py:114
  92.5 6.1 copy.298
  98.6 11.6 %slice.451 = bf16[2,4,5120]{2,1,0:T(4,128)(2,1)S(1)} reshape(bf16[2,320,32,2]{3,2,1,0:T(8,128)(2,1)} %copy.298) | data formatting | bytes 163840 | tf_op jit(solution)/shard_map/slice | solution.py:64
  110.2 4.5 collective-permute-start
  122.3 3.0 add.168
  125.3 6.8 add.169
  133.3 3.0 mul.338
  136.3 6.8 mul.339
  144.4 3.2 add.155
  147.6 6.8 add.156
  154.3 3.0 mul.317
  157.3 6.8 mul.318
  164.1 6.1 sub.92.clone
  170.2 6.0 copy.300
  176.3 6.1 mul.309.clone
  182.4 6.1 copy.302
  193.8 3.0 collective-permute-start.1
  205.2 3.8 concatenate.70
  211.3 4.8 concatenate.72
  216.2 2.9 convolution_add_fusion.7
  219.1 4.9 concatenate.73
  223.9 2.9 fusion.1
  235.9 4.8 concatenate.81
  240.8 2.8 fusion.95
  243.6 4.8 concatenate.83
  248.4 2.9 convolution_add_fusion.3
  251.3 4.5 concatenate.84
  260.1 2.7 copy.358
  262.8 2.7 copy.357
  266.2 39.6 %all-reduce.6 = (f32[8,32]{1,0:T(8,128)S(1)}, f32[8,32]{1,0:T(8,128)S(1)}) all-reduce(f32[8,32]{1,0:T(8,128)S(1)} %fusion.45, f32[8,32]{1,0:T(8,128)S(1)} %fusion.47), channel_id=1, replica_groups=mesh['tm'=16,'rows'=2] {'tm','rows'}, use_global_device_ids=true, to_apply=%region_8.9 | all-reduce | flops 512 | bytes 4096 | tf_op jit(solution)/shard_map/psum | solution.py:114
  312.7 39.9 %all-reduce.5 = (f32[8,32]{1,0:T(8,128)S(1)}, f32[8,32]{1,0:T(8,128)S(1)}) all-reduce(f32[8,32]{1,0:T(8,128)S(1)} %fusion.41, f32[8,32]{1,0:T(8,128)S(1)} %fusion.43), channel_id=1, replica_groups=mesh['tm'=16,'rows'=2] {'tm','rows'}, use_global_device_ids=true, to_apply=%region_12.13 | all-reduce | flops 512 | bytes 4096 | tf_op jit(solution)/shard_map/psum | solution.py:114
  360.0 6.1 copy.310
  366.1 11.5 %slice.491 = bf16[2,4,5120]{2,1,0:T(4,128)(2,1)S(1)} reshape(bf16[2,320,32,2]{3,2,1,0:T(8,128)(2,1)} %copy.310) | data formatting | bytes 163840 | tf_op jit(solution)/shard_map/slice | solution.py:64
  377.6 4.4 collective-permute-start.4
  382.0 6.2 sub.104
  388.2 6.0 copy.328
  394.2 6.2 mul.360
  400.4 6.0 copy.331
  406.4 6.2 mul.330.clone
  412.6 6.0 copy.315
  418.6 6.2 sub.97.clone
  424.7 6.1 copy.313
  433.6 4.1 collective-permute-done.11
  439.3 3.0 collective-permute-start.12
  444.6 4.3 collective-permute-start.5
  455.4 3.8 concatenate.87
  461.5 3.8 concatenate.88
  465.4 2.4 convolution_add_fusion.1
  467.8 3.4 concatenate.89
  480.0 3.7 concatenate.78
  487.3 41.4 %all-reduce.4 = (f32[8,32]{1,0:T(8,128)S(1)}, f32[8,32]{1,0:T(8,128)S(1)}) all-reduce(f32[8,32]{1,0:T(8,128)S(1)} %fusion.37, f32[8,32]{1,0:T(8,128)S(1)} %fusion.39), channel_id=1, replica_groups=mesh['tm'=16,'rows'=2] {'tm','rows'}, use_global_device_ids=true, to_apply=%region_16.17 | all-reduce | flops 512 | bytes 4096 | tf_op jit(solution)/shard_map/psum | solution.py:114
  532.9 4.7 concatenate.77
  537.6 2.7 copy.361
  540.3 2.8 convolution_bitcast_fusion
  545.8 4.7 concatenate.76
  559.5 6.1 mul.376
  565.6 6.0 copy.347
  571.6 6.1 sub.110
  577.8 6.1 copy.344
  586.9 130.3 %all-reduce.11.cloned.1.call-done = (f32[3,3,3,64,64]{4,3,2,1,0:T(8,128)}, f32[3,3,3,64,64]{4,3,2,1,0:T(8,128)}) async-done(((f32[3,3,3,64,64]{4,3,2,1,0:T(8,128)}, f32[3,3,3,64,64]{4,3,2,1,0:T(8,128)}), (f32[3,3,3,64,64]{4,3,2,1,0:T(8,128)}, f32[3,3,3,64,64]{4,3,2,1,0:T(8,128)})) %all-reduce.11.cloned.1.call-update) | async-done | bytes 884752 | tf_op jit(solution)/shard_map/psum | solution.py:189
  (319 shorter events, 111.1 us)
Async XLA Ops:
  7.2 710.1 %all-reduce.11.cloned.1.call-start = ((), (), s32[]{:S(2)}) async-start(), calls=%async_computation | async-start | bytes 3538944 | tf_op jit(solution)/shard_map/psum | solution.py:189
  7.9 180.8 %collective-permute-start.10 = (bf16[2]{0:T(256)(128)(2,1)S(1)}, bf16[2]{0:T(256)(128)(2,1)S(1)}, u32[]{:S(2)}, u32[]{:S(2)}) collective-permute-start(bf16[2]{0:T(256)(128)(2,1)S(1)} %get-tuple-element.192), channel_id=1, source_target_pairs={{2,0},{4,2},{6,4},{8,6},{10,8},{12,10},{14,12},{16,14},{18,16},{20... | collective-permute-start | bytes 20 | tf_op jit(solution)/shard_map/ppermute | solution.py:27
  9.2 179.5 %collective-permute-start.3 = (bf16[2]{0:T(256)(128)(2,1)S(1)}, bf16[2]{0:T(256)(128)(2,1)S(1)}, u32[]{:S(2)}, u32[]{:S(2)}) collective-permute-start(bf16[2]{0:T(256)(128)(2,1)S(1)} %get-tuple-element.193), channel_id=1, source_target_pairs={{0,2},{2,4},{4,6},{6,8},{8,10},{10,12},{12,14},{14,16},{16,18},{18... | collective-permute-start | bytes 20 | tf_op jit(solution)/shard_map/ppermute | solution.py:27
  15.6 173.3 %collective-permute-start.7 = (bf16[2,4,5120]{2,1,0:T(4,128)(2,1)S(1)}, bf16[2,4,5120]{2,1,0:T(4,128)(2,1)S(1)}, u32[]{:S(2)}, u32[]{:S(2)}) collective-permute-start(bf16[2,4,5120]{2,1,0:T(4,128)(2,1)S(1)} %slice.527), channel_id=1, source_target_pairs={{2,0},{4,2},{6,4},{8,6},{10,8},{12,10},{14,12},{16,14},{18,16},{20... | collective-permute-start | bytes 245768 | tf_op jit(solution)/shard_map/ppermute | solution.py:27
  34.6 10.3 %copy-start.67 = (f32[64]{0:T(128)S(1)}, f32[64]{0:T(128)}, u32[]{:S(2)}) copy-start(f32[64]{0:T(128)} %param.13) | copy-start | bytes 772
  34.7 10.5 %copy-start.68 = (f32[64]{0:T(128)S(1)}, f32[64]{0:T(128)}, u32[]{:S(2)}) copy-start(f32[64]{0:T(128)} %param.14) | copy-start | bytes 772
  34.7 10.6 %copy-start.71 = (s32[4]{0:T(128)S(1)}, s32[4]{0:T(128)}, u32[]{:S(2)}) copy-start(s32[4]{0:T(128)} %param.17) | copy-start | bytes 52
  44.9 53.7 %copy-start.11 = (f32[4,320,32,2]{1,2,3,0:T(8,128)}, f32[4,320,32,2]{1,2,3,0:T(8,128)S(1)}, u32[]{:S(2)}) copy-start(f32[4,320,32,2]{1,2,3,0:T(8,128)S(1)} %copy.295) | copy-start | bytes 983044
  45.1 46.6 %copy-start.55 = (f32[32,2]{0,1:T(2,128)}, f32[32,2]{0,1:T(2,128)S(1)}, u32[]{:S(2)}) copy-start(f32[32,2]{0,1:T(2,128)S(1)} %copy.296) | copy-start | bytes 772
  91.0 261.8 %copy-start.73 = (f32[4]{0:T(128)}, f32[4]{0:T(128)S(1)}, u32[]{:S(2)}) copy-start(f32[4]{0:T(128)S(1)} %fusion.8) | copy-start | bytes 52
  91.2 24.7 %copy-start.51 = (f32[4,32]{1,0:T(4,128)}, f32[4,32]{1,0:T(4,128)S(1)}, u32[]{:S(2)}) copy-start(f32[4,32]{1,0:T(4,128)S(1)} %convolution_divide_fusion.7) | copy-start | bytes 1540
  91.4 24.4 %copy-start.53 = (f32[4,32]{1,0:T(4,128)}, f32[4,32]{1,0:T(4,128)S(1)}, u32[]{:S(2)}) copy-start(f32[4,32]{1,0:T(4,128)S(1)} %fusion.7) | copy-start | bytes 1540
  98.6 16.1 %copy-start.21 = (bf16[4,4,5120]{2,1,0:T(4,128)(2,1)S(1)}, bf16[4,4,5120]{2,1,0:T(4,128)(2,1)}, u32[]{:S(2)}) copy-start(bf16[4,4,5120]{2,1,0:T(4,128)(2,1)} %param.10) | copy-start | bytes 491524
  98.6 17.3 %copy-start.69 = (f32[64]{0:T(128)S(1)}, f32[64]{0:T(128)}, u32[]{:S(2)}) copy-start(f32[64]{0:T(128)} %param.15) | copy-start | bytes 772
  98.6 17.5 %copy-start.70 = (f32[64]{0:T(128)S(1)}, f32[64]{0:T(128)}, u32[]{:S(2)}) copy-start(f32[64]{0:T(128)} %param.16) | copy-start | bytes 772
  98.6 17.7 %copy-start.47 = (bf16[3,3,3,64,64]{4,3,2,1,0:T(8,128)(2,1)S(1)}, bf16[3,3,3,64,64]{4,3,2,1,0:T(8,128)(2,1)}, u32[]{:S(2)}) copy-start(bf16[3,3,3,64,64]{4,3,2,1,0:T(8,128)(2,1)} %param.11) | copy-start | bytes 663556
  110.2 9.4 %copy-start.48 = (bf16[3,3,3,64,64]{4,3,2,1,0:T(8,128)(2,1)S(1)}, bf16[3,3,3,64,64]{4,3,2,1,0:T(8,128)(2,1)}, u32[]{:S(2)}) copy-start(bf16[3,3,3,64,64]{4,3,2,1,0:T(8,128)(2,1)} %param.12) | copy-start | bytes 663556
  110.2 81.6 %collective-permute-start = (bf16[2,4,5120]{2,1,0:T(4,128)(2,1)S(1)}, bf16[2,4,5120]{2,1,0:T(4,128)(2,1)S(1)}, u32[]{:S(2)}, u32[]{:S(2)}) collective-permute-start(bf16[2,4,5120]{2,1,0:T(4,128)(2,1)S(1)} %slice.451), channel_id=1, source_target_pairs={{0,2},{2,4},{4,6},{6,8},{8,10},{10,12},{12,14},{14,16},{16,18},{18... | collective-permute-start | bytes 245768 | tf_op jit(solution)/shard_map/ppermute | solution.py:27
  143.1 4.5 copy-start.40
  154.3 34.1 %copy-start.36 = (f32[4,5120]{1,0:T(4,128)}, f32[4,5120]{1,0:T(4,128)S(1)}, u32[]{:S(2)}) copy-start(f32[4,5120]{1,0:T(4,128)S(1)} %add.156) | copy-start | bytes 245764
  164.1 24.4 %copy-start.38 = (f32[4,5120]{1,0:T(4,128)}, f32[4,5120]{1,0:T(4,128)S(1)}, u32[]{:S(2)}) copy-start(f32[4,5120]{1,0:T(4,128)S(1)} %mul.318) | copy-start | bytes 245764
  176.2 12.2 %copy-start.13 = (f32[4,4,5120]{2,1,0:T(4,128)}, f32[4,4,5120]{2,1,0:T(4,128)S(1)}, u32[]{:S(2)}) copy-start(f32[4,4,5120]{2,1,0:T(4,128)S(1)} %copy.300) | copy-start | bytes 983044
  182.4 6.1 copy-start.24
  188.5 8.8 %copy-start.15 = (f32[4,4,5120]{2,1,0:T(4,128)}, f32[4,4,5120]{2,1,0:T(4,128)S(1)}, u32[]{:S(2)}) copy-start(f32[4,4,5120]{2,1,0:T(4,128)S(1)} %copy.302) | copy-start | bytes 983044
  188.9 10.0 %copy-start.57 = (bf16[4]{0:T(256)(128)(2,1)}, bf16[4]{0:T(256)(128)(2,1)S(1)}, u32[]{:S(2)}) copy-start(bf16[4]{0:T(256)(128)(2,1)S(1)} %get-tuple-element.187) | copy-start | bytes 28
  188.9 10.0 %copy-start.59 = (bf16[4]{0:T(256)(128)(2,1)}, bf16[4]{0:T(256)(128)(2,1)S(1)}, u32[]{:S(2)}) copy-start(bf16[4]{0:T(256)(128)(2,1)S(1)} %get-tuple-element.188) | copy-start | bytes 28
  188.9 10.0 %copy-start.61 = (bf16[4]{0:T(256)(128)(2,1)}, bf16[4]{0:T(256)(128)(2,1)S(1)}, u32[]{:S(2)}) copy-start(bf16[4]{0:T(256)(128)(2,1)S(1)} %get-tuple-element.189) | copy-start | bytes 28
  189.0 10.0 %copy-start.63 = (bf16[4]{0:T(256)(128)(2,1)}, bf16[4]{0:T(256)(128)(2,1)S(1)}, u32[]{:S(2)}) copy-start(bf16[4]{0:T(256)(128)(2,1)S(1)} %get-tuple-element.183) | copy-start | bytes 28
  189.0 10.0 %copy-start.65 = (bf16[4]{0:T(256)(128)(2,1)}, bf16[4]{0:T(256)(128)(2,1)S(1)}, u32[]{:S(2)}) copy-start(bf16[4]{0:T(256)(128)(2,1)S(1)} %get-tuple-element.184) | copy-start | bytes 28
  189.2 7.7 %collective-permute-start.8 = (bf16[6,1,5120]{2,1,0:T(2,128)(2,1)S(1)}, bf16[6,1,5120]{2,1,0:T(2,128)(2,1)S(1)}, u32[]{:S(2)}, u32[]{:S(2)}) collective-permute-start(bf16[6,1,5120]{2,1,0:T(2,128)(2,1)S(1)} %get-tuple-element.177), channel_id=1, source_target_pairs={{0,1},{2,3},{4,5},{6,7},{8,9},{10,11},{12,13},{14,15},{16,17},{18,... | collective-permute-start | bytes 184328 | tf_op jit(solution)/shard_map/ppermute | solution.py:16
  190.5 6.4 collective-permute-start.9
  192.1 5.7 collective-permute-start.2
  193.8 4.1 collective-permute-start.1
  235.9 4.9 copy-start.43
  240.8 2.9 copy-start.27
  243.6 4.8 copy-start.42
  248.4 2.9 copy-start.26
  262.8 2.7 copy-start.2
  265.5 43.2 %copy-start.17 = (f32[1280,64]{1,0:T(8,128)S(1)}, f32[1280,64]{1,0:T(8,128)}, u32[]{:S(2)}) copy-start(f32[1280,64]{1,0:T(8,128)} %copy.311) | copy-start | bytes 983044
  311.8 43.6 %copy-start.7 = (f32[1280,64]{0,1:T(8,128)S(1)}, f32[1280,64]{0,1:T(8,128)}, u32[]{:S(2)}) copy-start(f32[1280,64]{0,1:T(8,128)} %fusion.1) | copy-start | bytes 983044
  311.8 43.6 %copy-start.9 = (f32[1280,64]{0,1:T(8,128)S(1)}, f32[1280,64]{0,1:T(8,128)}, u32[]{:S(2)}) copy-start(f32[1280,64]{0,1:T(8,128)} %copy-done.8) | copy-start | bytes 983044
  311.9 43.6 %copy-start.29 = (f32[1280,64]{0,1:T(8,128)S(1)}, f32[1280,64]{0,1:T(8,128)}, u32[]{:S(2)}) copy-start(f32[1280,64]{0,1:T(8,128)} %sub.114) | copy-start | bytes 983044
  377.6 64.7 %collective-permute-start.4 = (bf16[2,4,5120]{2,1,0:T(4,128)(2,1)S(1)}, bf16[2,4,5120]{2,1,0:T(4,128)(2,1)S(1)}, u32[]{:S(2)}, u32[]{:S(2)}) collective-permute-start(bf16[2,4,5120]{2,1,0:T(4,128)(2,1)S(1)} %slice.491), channel_id=1, source_target_pairs={{0,2},{2,4},{4,6},{6,8},{8,10},{10,12},{12,14},{14,16},{16,18},{18... | collective-permute-start | bytes 245768 | tf_op jit(solution)/shard_map/ppermute | solution.py:27
  424.7 6.1 copy-start.28
  424.7 6.1 copy-start.41
  431.3 6.3 collective-permute-start.11
  438.0 10.9 %collective-permute-start.13 = (bf16[6,1,5120]{2,0,1:T(8,128)(2,1)S(1)}, bf16[6,1,5120]{2,0,1:T(8,128)(2,1)S(1)}, u32[]{:S(2)}, u32[]{:S(2)}) collective-permute-start(bf16[6,1,5120]{2,0,1:T(8,128)(2,1)S(1)} %copy.334), channel_id=1, source_target_pairs={{1,0},{3,2},{5,4},{7,6},{9,8},{11,10},{13,12},{15,14},{17,16},{19,... | collective-permute-start | bytes 184328 | tf_op jit(solution)/shard_map/ppermute | solution.py:19
  439.3 9.7 %collective-permute-start.12 = (bf16[6,1,5120]{2,0,1:T(8,128)(2,1)S(1)}, bf16[6,1,5120]{2,0,1:T(8,128)(2,1)S(1)}, u32[]{:S(2)}, u32[]{:S(2)}) collective-permute-start(bf16[6,1,5120]{2,0,1:T(8,128)(2,1)S(1)} %copy.333), channel_id=1, source_target_pairs={{0,1},{2,3},{4,5},{6,7},{8,9},{10,11},{12,13},{14,15},{16,17},{18,... | collective-permute-start | bytes 184328 | tf_op jit(solution)/shard_map/ppermute | solution.py:16
  442.3 7.7 %copy-start.49 = (bf16[2,4,5120]{2,1,0:T(4,128)(2,1)}, bf16[2,4,5120]{2,1,0:T(4,128)(2,1)S(1)}, u32[]{:S(2)}) copy-start(bf16[2,4,5120]{2,1,0:T(4,128)(2,1)S(1)} %collective-permute-done.4) | copy-start | bytes 245764
  442.5 7.4 %copy-start.58 = (bf16[4]{0:T(256)(128)(2,1)S(1)}, bf16[4]{0:T(256)(128)(2,1)}, u32[]{:S(2)}) copy-start(bf16[4]{0:T(256)(128)(2,1)} %copy-done.57) | copy-start | bytes 28
  442.5 7.4 %copy-start.64 = (bf16[4]{0:T(256)(128)(2,1)S(1)}, bf16[4]{0:T(256)(128)(2,1)}, u32[]{:S(2)}) copy-start(bf16[4]{0:T(256)(128)(2,1)} %copy-done.63) | copy-start | bytes 28
  442.6 7.4 %copy-start.66 = (bf16[4]{0:T(256)(128)(2,1)S(1)}, bf16[4]{0:T(256)(128)(2,1)}, u32[]{:S(2)}) copy-start(bf16[4]{0:T(256)(128)(2,1)} %copy-done.65) | copy-start | bytes 28
  443.3 31.8 %collective-permute-start.6 = (bf16[6,1,5120]{2,0,1:T(8,128)(2,1)}, bf16[6,1,5120]{2,0,1:T(8,128)(2,1)}, u32[]{:S(2)}, u32[]{:S(2)}) collective-permute-start(bf16[6,1,5120]{2,0,1:T(8,128)(2,1)} %copy.379), channel_id=1, source_target_pairs={{1,0},{3,2},{5,4},{7,6},{9,8},{11,10},{13,12},{15,14},{17,16},{19,... | collective-permute-start | bytes 184328 | tf_op jit(solution)/shard_map/ppermute | solution.py:19
  444.6 31.5 %collective-permute-start.5 = (bf16[6,1,5120]{2,0,1:T(8,128)(2,1)S(1)}, bf16[6,1,5120]{2,0,1:T(8,128)(2,1)}, u32[]{:S(2)}, u32[]{:S(2)}) collective-permute-start(bf16[6,1,5120]{2,0,1:T(8,128)(2,1)S(1)} %copy.378), channel_id=1, source_target_pairs={{0,1},{2,3},{4,5},{6,7},{8,9},{10,11},{12,13},{14,15},{16,17},{18,... | collective-permute-start | bytes 184328 | tf_op jit(solution)/shard_map/ppermute | solution.py:16
  472.9 4.1 copy-start.50
  474.0 4.0 copy-start.60
  474.0 4.0 copy-start.62
  483.7 3.1 copy-start.72
  483.8 45.0 %copy-start.74 = (f32[4]{0:T(128)S(1)}, f32[4]{0:T(128)}, u32[]{:S(2)}) copy-start(f32[4]{0:T(128)} %copy-done.73) | copy-start | bytes 52
  540.3 2.8 copy-start.6
  545.8 4.7 copy-start.46
  577.8 6.1 copy-start.32
  577.8 6.1 copy-start.33
  577.8 6.1 copy-start.34
  (26 other events, 44.3 us)
Sparse Core Ops, SparseCore 0:
  585.1 132.0 all-reduce.10
where the time goes:
time: 739 us; the launch traced here: 728 us
  local copies, waits for them, and re-layouts  314 us (42%)
  blocking collectives  166 us (22%)
  waiting for transfers between devices  134 us (18%)
  matrix products  38 us (5%)
  starting transfers between devices  35.5 us (5%)
  other arithmetic  24.3 us (3%)
  between operations  15.8 us (2%)
    psum x4, blocking collectives, clip_totals(): lax.psum((table_a, table_b, table_c), ('tm', 'rows'))  166 us
    psum x1, waiting for transfers between devices, per_device(): grad_one, grad_two = lax.psum((grad_one, grad_two), ('tm', 'rows'))  130 us
    slice x4, local copies, waits for them, and re-layouts, causal_conv(): past_field, past_tags = passed_along((field[-2:], tags[-2:]), 'tm', 1)  35.3 us
    concatenate x6, local copies, waits for them, and re-layouts, forward_taps(): joined = jnp.concatenate(taps, axis=-1)  26.6 us
    sub x6, local copies, waits for them, and re-layouts, norm_backward(): grad_norm - p_term[:, None, :, None] - normed * q_term[:, None, :, None]  25.6 us
    mul x6, local copies, waits for them, and re-layouts, norm_forward(): normed = (grouped - mean_val[:, None, :, None]) * inv_std[:, None, :, None]  25.5 us
    sub x6, local copies, waits for them, and re-layouts, norm_forward(): normed = (grouped - mean_val[:, None, :, None]) * inv_std[:, None, :, None]  25.5 us
    mul x6, local copies, waits for them, and re-layouts, norm_backward(): normed * q_term[:, None, :, None]  25.4 us
  transfers between devices with their start and end apart: 15, of which 2 were waited for; matrix products, arithmetic and copies ran while one was open for 28% of the time, Pallas kernels for 0%

commit v1 on v0

--- a/solution.py
+++ b/solution.py
@@ -186,7 +186,7 @@
     back_one = transposed_conv(grad_hidden, tags, kernel_one)
     branch = norm_backward(back_one, normed_one, z_one, inv_one, cells_count, gain_one, clip_id)
     grad_latent = (cotangent.astype(jnp.float32) + branch).astype(jnp.bfloat16)
-    grad_one, grad_two = lax.psum((grad_one, grad_two), ("tm", "rows"))
+    grad_one, grad_two = lax.psum(lax.psum((grad_one, grad_two), "rows"), "tm")
     return (output, grad_latent, grad_one, grad_two)
 
 

time: 739 us -> 723 us (0.978)
  waiting for transfers between devices: 134 us -> 122 us
    psum x1 -> x2, waiting for transfers between devices: 130 us -> 118 us  [per_device(): grad_one, grad_two = lax.psum(lax.psum((grad_one, grad_two), 'rows'), 'tm')]
  transfers between devices with their start and end apart: 15 -> 16, of which waited for: 2 -> 2; matrix products, arithmetic and copies ran while one was open for 28% -> 29% of each run, Pallas kernels for 0% -> 0%
where the time goes in v1:
time: 723 us; the launch traced here: 711 us
  local copies, waits for them, and re-layouts  310 us (43%)
  blocking collectives  166 us (23%)
  waiting for transfers between devices  122 us (17%)
  matrix products  37.9 us (5%)
  starting transfers between devices  34.3 us (5%)
  other arithmetic  24.4 us (3%)
  between operations  15.8 us (2%)
    psum x4, blocking collectives, clip_totals(): lax.psum((table_a, table_b, table_c), ('tm', 'rows'))  166 us
    psum x2, waiting for transfers between devices, per_device(): grad_one, grad_two = lax.psum(lax.psum((grad_one, grad_two), 'rows'), 'tm')  118 us
    slice x4, local copies, waits for them, and re-layouts, causal_conv(): past_field, past_tags = passed_along((field[-2:], tags[-2:]), 'tm', 1)  35.9 us
    concatenate x6, local copies, waits for them, and re-layouts, forward_taps(): joined = jnp.concatenate(taps, axis=-1)  26.7 us
    mul x6, local copies, waits for them, and re-layouts, norm_backward(): normed * q_term[:, None, :, None]  25.7 us
    sub x6, local copies, waits for them, and re-layouts, norm_forward(): normed = (grouped - mean_val[:, None, :, None]) * inv_std[:, None, :, None]  25.6 us
    mul x6, local copies, waits for them, and re-layouts, norm_forward(): normed = (grouped - mean_val[:, None, :, None]) * inv_std[:, None, :, None]  25.6 us
    concatenate x6, local copies, waits for them, and re-layouts, reverse_taps(): joined = jnp.concatenate(taps, axis=-1)  25.5 us
  transfers between devices with their start and end apart: 16, of which 2 were waited for; matrix products, arithmetic and copies ran while one was open for 29% of the time, Pallas kernels for 0%

profile of v1, /device:TPU:0, one launch (start us, length us, event | category | flops | bytes accessed | tf_op | source)
XLA Modules:
  0.0 711.1 jit_solution(15396793295443986345)
XLA Ops:
  9.2 5.5 collective-permute-start.3
  17.8 5.7 copy.294
  23.5 11.2 %fusion.74 = (f32[4,32]{0,1:T(8,128)S(1)}, f32[4,32]{0,1:T(8,128)S(1)}) fusion(f32[4,320,32,2]{0,3,2,1:T(2,128)} %bitcast.178), kind=kLoop, calls=%fused_computation.168 | loop fusion | flops 245504 | bytes 328704 | tf_op jit(solution)/shard_map/reduce_sum | solution.py:127
  34.7 10.2 %copy.295 = f32[4,320,32,2]{1,2,3,0:T(8,128)S(1)} copy(f32[4,320,32,2]{0,3,2,1:T(2,128)} %bitcast.179) | data formatting | bytes 655360 | tf_op jit(solution)/shard_map/reshape | solution.py:126
  45.9 45.0 %all-reduce.7 = (f32[8,32]{1,0:T(8,128)S(1)}, f32[8,32]{1,0:T(8,128)S(1)}, f32[8]{0:T(128)S(1)}) all-reduce(f32[8,32]{1,0:T(8,128)S(1)} %fusion.49, f32[8,32]{1,0:T(8,128)S(1)} %fusion.51, f32[8]{0:T(128)S(1)} %convolution_bitcast_fusion.7), channel_id=1, replica_groups=mesh['tm'=16,'rows'=2] {'tm','rows'}, use_global_device_ids=true, to_apply=%region_4.0 | all-reduce | flops 520 | bytes 4160 | tf_op jit(solution)/shard_map/psum | solution.py:114
  92.6 6.1 copy.298
  98.7 11.6 %slice.451 = bf16[2,4,5120]{2,1,0:T(4,128)(2,1)S(1)} reshape(bf16[2,320,32,2]{3,2,1,0:T(8,128)(2,1)} %copy.298) | data formatting | bytes 163840 | tf_op jit(solution)/shard_map/slice | solution.py:64
  110.3 4.5 collective-permute-start
  122.3 3.0 add.172
  125.3 6.8 add.173
  133.4 3.0 mul.338
  136.4 6.8 mul.339
  144.5 3.2 add.159
  147.6 6.8 add.160
  154.4 3.0 mul.317
  157.4 6.8 mul.318
  164.1 6.1 sub.92.clone
  170.3 6.0 copy.300
  176.3 6.1 mul.309.clone
  182.5 6.1 copy.302
  193.9 3.0 collective-permute-start.1
  205.3 3.8 concatenate.70
  211.4 4.8 concatenate.72
  216.2 2.9 convolution_add_fusion.7
  219.2 4.9 concatenate.73
  224.0 2.9 fusion.1
  236.0 4.9 concatenate.81
  240.9 2.8 fusion.95
  243.8 4.8 concatenate.83
  248.6 2.9 convolution_add_fusion.3
  251.5 4.5 concatenate.84
  260.2 2.7 copy.358
  262.9 2.7 copy.357
  266.3 39.6 %all-reduce.6 = (f32[8,32]{1,0:T(8,128)S(1)}, f32[8,32]{1,0:T(8,128)S(1)}) all-reduce(f32[8,32]{1,0:T(8,128)S(1)} %fusion.45, f32[8,32]{1,0:T(8,128)S(1)} %fusion.47), channel_id=1, replica_groups=mesh['tm'=16,'rows'=2] {'tm','rows'}, use_global_device_ids=true, to_apply=%region_8.9 | all-reduce | flops 512 | bytes 4096 | tf_op jit(solution)/shard_map/psum | solution.py:114
  312.7 39.9 %all-reduce.5 = (f32[8,32]{1,0:T(8,128)S(1)}, f32[8,32]{1,0:T(8,128)S(1)}) all-reduce(f32[8,32]{1,0:T(8,128)S(1)} %fusion.41, f32[8,32]{1,0:T(8,128)S(1)} %fusion.43), channel_id=1, replica_groups=mesh['tm'=16,'rows'=2] {'tm','rows'}, use_global_device_ids=true, to_apply=%region_12.13 | all-reduce | flops 512 | bytes 4096 | tf_op jit(solution)/shard_map/psum | solution.py:114
  360.1 6.1 copy.310
  366.2 12.1 %slice.491 = bf16[2,4,5120]{2,1,0:T(4,128)(2,1)} reshape(bf16[2,320,32,2]{3,2,1,0:T(8,128)(2,1)} %copy.310) | data formatting | bytes 163840 | tf_op jit(solution)/shard_map/slice | solution.py:64
  378.3 4.4 collective-permute-start.4
  382.7 6.2 sub.104
  388.9 6.0 copy.328
  394.9 6.2 mul.360
  401.1 6.0 copy.331
  407.1 6.2 mul.330.clone
  413.3 6.0 copy.315
  419.3 6.2 sub.97.clone
  425.5 6.1 copy.313
  434.4 4.1 collective-permute-done.11
  440.1 3.0 collective-permute-start.12
  444.7 3.0 collective-permute-start.5
  454.3 4.7 concatenate.78
  459.0 2.7 copy.363
  465.1 3.8 concatenate.87
  471.3 3.8 concatenate.88
  477.5 3.7 concatenate.89
  485.2 41.4 %all-reduce.4 = (f32[8,32]{1,0:T(8,128)S(1)}, f32[8,32]{1,0:T(8,128)S(1)}) all-reduce(f32[8,32]{1,0:T(8,128)S(1)} %fusion.37, f32[8,32]{1,0:T(8,128)S(1)} %fusion.39), channel_id=1, replica_groups=mesh['tm'=16,'rows'=2] {'tm','rows'}, use_global_device_ids=true, to_apply=%region_16.17 | all-reduce | flops 512 | bytes 4096 | tf_op jit(solution)/shard_map/psum | solution.py:114
  528.3 3.7 concatenate.77
  533.7 2.7 convolution_bitcast_fusion
  539.4 4.8 concatenate.76
  544.1 2.7 copy.359
  555.4 6.2 mul.376
  561.6 6.2 copy.347
  567.8 6.2 sub.110
  573.9 6.0 copy.344
  582.4 118.3 %all-reduce.13.cloned.1.call-done = (f32[3,3,3,64,64]{4,3,2,1,0:T(8,128)}, f32[3,3,3,64,64]{4,3,2,1,0:T(8,128)}) async-done(((f32[3,3,3,64,64]{4,3,2,1,0:T(8,128)}, f32[3,3,3,64,64]{4,3,2,1,0:T(8,128)}), (f32[3,3,3,64,64]{4,3,2,1,0:T(8,128)}, f32[3,3,3,64,64]{4,3,2,1,0:T(8,128)})) %all-reduce.13.cloned.1.call-update) | async-done | bytes 884752 | tf_op jit(solution)/shard_map/psum | solution.py:189
  (312 shorter events, 106.2 us)
Async XLA Ops:
  7.2 572.9 %all-reduce.15.cloned.1.call-start = ((), (), s32[]{:S(2)}) async-start(), calls=%async_computation.1 | async-start | bytes 3538944 | tf_op jit(solution)/shard_map/psum | solution.py:189
  7.9 180.9 %collective-permute-start.10 = (bf16[2]{0:T(256)(128)(2,1)S(1)}, bf16[2]{0:T(256)(128)(2,1)S(1)}, u32[]{:S(2)}, u32[]{:S(2)}) collective-permute-start(bf16[2]{0:T(256)(128)(2,1)S(1)} %get-tuple-element.194), channel_id=1, source_target_pairs={{2,0},{4,2},{6,4},{8,6},{10,8},{12,10},{14,12},{16,14},{18,16},{20... | collective-permute-start | bytes 20 | tf_op jit(solution)/shard_map/ppermute | solution.py:27
  9.2 179.6 %collective-permute-start.3 = (bf16[2]{0:T(256)(128)(2,1)S(1)}, bf16[2]{0:T(256)(128)(2,1)S(1)}, u32[]{:S(2)}, u32[]{:S(2)}) collective-permute-start(bf16[2]{0:T(256)(128)(2,1)S(1)} %get-tuple-element.195), channel_id=1, source_target_pairs={{0,2},{2,4},{4,6},{6,8},{8,10},{10,12},{12,14},{14,16},{16,18},{18... | collective-permute-start | bytes 20 | tf_op jit(solution)/shard_map/ppermute | solution.py:27
  15.6 173.4 %collective-permute-start.7 = (bf16[2,4,5120]{2,1,0:T(4,128)(2,1)S(1)}, bf16[2,4,5120]{2,1,0:T(4,128)(2,1)S(1)}, u32[]{:S(2)}, u32[]{:S(2)}) collective-permute-start(bf16[2,4,5120]{2,1,0:T(4,128)(2,1)S(1)} %slice.527), channel_id=1, source_target_pairs={{2,0},{4,2},{6,4},{8,6},{10,8},{12,10},{14,12},{16,14},{18,16},{20... | collective-permute-start | bytes 245768 | tf_op jit(solution)/shard_map/ppermute | solution.py:27
  34.7 10.3 %copy-start.62 = (f32[64]{0:T(128)S(1)}, f32[64]{0:T(128)}, u32[]{:S(2)}) copy-start(f32[64]{0:T(128)} %param.13) | copy-start | bytes 772
  34.7 10.5 %copy-start.63 = (f32[64]{0:T(128)S(1)}, f32[64]{0:T(128)}, u32[]{:S(2)}) copy-start(f32[64]{0:T(128)} %param.14) | copy-start | bytes 772
  34.7 10.6 %copy-start.66 = (s32[4]{0:T(128)S(1)}, s32[4]{0:T(128)}, u32[]{:S(2)}) copy-start(s32[4]{0:T(128)} %param.17) | copy-start | bytes 52
  45.0 53.7 %copy-start.10 = (f32[4,320,32,2]{1,2,3,0:T(8,128)}, f32[4,320,32,2]{1,2,3,0:T(8,128)S(1)}, u32[]{:S(2)}) copy-start(f32[4,320,32,2]{1,2,3,0:T(8,128)S(1)} %copy.295) | copy-start | bytes 983044
  45.2 46.6 %copy-start.50 = (f32[32,2]{0,1:T(2,128)}, f32[32,2]{0,1:T(2,128)S(1)}, u32[]{:S(2)}) copy-start(f32[32,2]{0,1:T(2,128)S(1)} %copy.296) | copy-start | bytes 772
  91.1 261.8 %copy-start.68 = (f32[4]{0:T(128)}, f32[4]{0:T(128)S(1)}, u32[]{:S(2)}) copy-start(f32[4]{0:T(128)S(1)} %fusion.8) | copy-start | bytes 52
  91.3 24.7 %copy-start.46 = (f32[4,32]{1,0:T(4,128)}, f32[4,32]{1,0:T(4,128)S(1)}, u32[]{:S(2)}) copy-start(f32[4,32]{1,0:T(4,128)S(1)} %convolution_divide_fusion.7) | copy-start | bytes 1540
  91.5 24.4 %copy-start.48 = (f32[4,32]{1,0:T(4,128)}, f32[4,32]{1,0:T(4,128)S(1)}, u32[]{:S(2)}) copy-start(f32[4,32]{1,0:T(4,128)S(1)} %fusion.7) | copy-start | bytes 1540
  98.7 16.1 %copy-start.19 = (bf16[4,4,5120]{2,1,0:T(4,128)(2,1)S(1)}, bf16[4,4,5120]{2,1,0:T(4,128)(2,1)}, u32[]{:S(2)}) copy-start(bf16[4,4,5120]{2,1,0:T(4,128)(2,1)} %param.10) | copy-start | bytes 491524
  98.7 17.3 %copy-start.64 = (f32[64]{0:T(128)S(1)}, f32[64]{0:T(128)}, u32[]{:S(2)}) copy-start(f32[64]{0:T(128)} %param.15) | copy-start | bytes 772
  98.7 17.5 %copy-start.65 = (f32[64]{0:T(128)S(1)}, f32[64]{0:T(128)}, u32[]{:S(2)}) copy-start(f32[64]{0:T(128)} %param.16) | copy-start | bytes 772
  98.7 17.7 %copy-start.42 = (bf16[3,3,3,64,64]{4,3,2,1,0:T(8,128)(2,1)S(1)}, bf16[3,3,3,64,64]{4,3,2,1,0:T(8,128)(2,1)}, u32[]{:S(2)}) copy-start(bf16[3,3,3,64,64]{4,3,2,1,0:T(8,128)(2,1)} %param.11) | copy-start | bytes 663556
  110.3 9.4 %copy-start.43 = (bf16[3,3,3,64,64]{4,3,2,1,0:T(8,128)(2,1)S(1)}, bf16[3,3,3,64,64]{4,3,2,1,0:T(8,128)(2,1)}, u32[]{:S(2)}) copy-start(bf16[3,3,3,64,64]{4,3,2,1,0:T(8,128)(2,1)} %param.12) | copy-start | bytes 663556
  110.3 81.6 %collective-permute-start = (bf16[2,4,5120]{2,1,0:T(4,128)(2,1)S(1)}, bf16[2,4,5120]{2,1,0:T(4,128)(2,1)S(1)}, u32[]{:S(2)}, u32[]{:S(2)}) collective-permute-start(bf16[2,4,5120]{2,1,0:T(4,128)(2,1)S(1)} %slice.451), channel_id=1, source_target_pairs={{0,2},{2,4},{4,6},{6,8},{8,10},{10,12},{12,14},{14,16},{16,18},{18... | collective-permute-start | bytes 245768 | tf_op jit(solution)/shard_map/ppermute | solution.py:27
  132.1 4.3 copy-start.33
  143.1 4.5 copy-start.35
  164.1 24.4 %copy-start.31 = (f32[4,5120]{1,0:T(4,128)}, f32[4,5120]{1,0:T(4,128)S(1)}, u32[]{:S(2)}) copy-start(f32[4,5120]{1,0:T(4,128)S(1)} %mul.318) | copy-start | bytes 245764
  176.3 12.2 %copy-start.12 = (f32[4,4,5120]{2,1,0:T(4,128)}, f32[4,4,5120]{2,1,0:T(4,128)S(1)}, u32[]{:S(2)}) copy-start(f32[4,4,5120]{2,1,0:T(4,128)S(1)} %copy.300) | copy-start | bytes 983044
  182.5 6.1 copy-start.22
  188.6 8.8 %copy-start.14 = (f32[4,4,5120]{2,1,0:T(4,128)}, f32[4,4,5120]{2,1,0:T(4,128)S(1)}, u32[]{:S(2)}) copy-start(f32[4,4,5120]{2,1,0:T(4,128)S(1)} %copy.302) | copy-start | bytes 983044
  189.0 10.0 %copy-start.52 = (bf16[4]{0:T(256)(128)(2,1)}, bf16[4]{0:T(256)(128)(2,1)S(1)}, u32[]{:S(2)}) copy-start(bf16[4]{0:T(256)(128)(2,1)S(1)} %get-tuple-element.189) | copy-start | bytes 28
  189.0 10.0 %copy-start.54 = (bf16[4]{0:T(256)(128)(2,1)}, bf16[4]{0:T(256)(128)(2,1)S(1)}, u32[]{:S(2)}) copy-start(bf16[4]{0:T(256)(128)(2,1)S(1)} %get-tuple-element.185) | copy-start | bytes 28
  189.0 10.0 %copy-start.56 = (bf16[4]{0:T(256)(128)(2,1)}, bf16[4]{0:T(256)(128)(2,1)S(1)}, u32[]{:S(2)}) copy-start(bf16[4]{0:T(256)(128)(2,1)S(1)} %get-tuple-element.186) | copy-start | bytes 28
  189.0 10.0 %copy-start.58 = (bf16[4]{0:T(256)(128)(2,1)}, bf16[4]{0:T(256)(128)(2,1)S(1)}, u32[]{:S(2)}) copy-start(bf16[4]{0:T(256)(128)(2,1)S(1)} %get-tuple-element.190) | copy-start | bytes 28
  189.0 10.0 %copy-start.60 = (bf16[4]{0:T(256)(128)(2,1)}, bf16[4]{0:T(256)(128)(2,1)S(1)}, u32[]{:S(2)}) copy-start(bf16[4]{0:T(256)(128)(2,1)S(1)} %get-tuple-element.191) | copy-start | bytes 28
  189.3 7.7 %collective-permute-start.8 = (bf16[6,1,5120]{2,1,0:T(2,128)(2,1)S(1)}, bf16[6,1,5120]{2,1,0:T(2,128)(2,1)S(1)}, u32[]{:S(2)}, u32[]{:S(2)}) collective-permute-start(bf16[6,1,5120]{2,1,0:T(2,128)(2,1)S(1)} %get-tuple-element.179), channel_id=1, source_target_pairs={{0,1},{2,3},{4,5},{6,7},{8,9},{10,11},{12,13},{14,15},{16,17},{18,... | collective-permute-start | bytes 184328 | tf_op jit(solution)/shard_map/ppermute | solution.py:16
  190.6 6.4 collective-permute-start.9
  192.2 5.7 collective-permute-start.2
  193.9 4.1 collective-permute-start.1
  236.0 4.9 copy-start.38
  240.9 2.9 copy-start.25
  243.8 4.8 copy-start.37
  248.6 2.9 copy-start.24
  258.1 2.1 copy-start.7
  262.9 2.7 copy-start.1
  265.6 43.2 %copy-start.16 = (f32[1280,64]{1,0:T(8,128)S(1)}, f32[1280,64]{1,0:T(8,128)}, u32[]{:S(2)}) copy-start(f32[1280,64]{1,0:T(8,128)} %copy.311) | copy-start | bytes 983044
  311.9 43.6 %copy-start.6 = (f32[1280,64]{0,1:T(8,128)S(1)}, f32[1280,64]{0,1:T(8,128)}, u32[]{:S(2)}) copy-start(f32[1280,64]{0,1:T(8,128)} %fusion.1) | copy-start | bytes 983044
  311.9 43.6 %copy-start.8 = (f32[1280,64]{0,1:T(8,128)S(1)}, f32[1280,64]{0,1:T(8,128)}, u32[]{:S(2)}) copy-start(f32[1280,64]{0,1:T(8,128)} %copy-done.7) | copy-start | bytes 983044
  311.9 43.6 %copy-start.27 = (f32[1280,64]{0,1:T(8,128)S(1)}, f32[1280,64]{0,1:T(8,128)}, u32[]{:S(2)}) copy-start(f32[1280,64]{0,1:T(8,128)} %sub.114) | copy-start | bytes 983044
  354.5 2.6 copy-start.3
  378.3 64.8 %collective-permute-start.4 = (bf16[2,4,5120]{2,1,0:T(4,128)(2,1)}, bf16[2,4,5120]{2,1,0:T(4,128)(2,1)S(1)}, u32[]{:S(2)}, u32[]{:S(2)}) collective-permute-start(bf16[2,4,5120]{2,1,0:T(4,128)(2,1)} %slice.491), channel_id=1, source_target_pairs={{0,2},{2,4},{4,6},{6,8},{8,10},{10,12},{12,14},{14,16},{16,18},{18... | collective-permute-start | bytes 245768 | tf_op jit(solution)/shard_map/ppermute | solution.py:27
  425.5 6.1 copy-start.26
  425.5 6.1 copy-start.34
  425.5 6.1 copy-start.36
  432.1 6.3 collective-permute-start.11
  438.8 9.0 %collective-permute-start.13 = (bf16[6,1,5120]{2,0,1:T(8,128)(2,1)S(1)}, bf16[6,1,5120]{2,0,1:T(8,128)(2,1)S(1)}, u32[]{:S(2)}, u32[]{:S(2)}) collective-permute-start(bf16[6,1,5120]{2,0,1:T(8,128)(2,1)S(1)} %copy.334), channel_id=1, source_target_pairs={{1,0},{3,2},{5,4},{7,6},{9,8},{11,10},{13,12},{15,14},{17,16},{19,... | collective-permute-start | bytes 184328 | tf_op jit(solution)/shard_map/ppermute | solution.py:19
  440.1 7.8 %collective-permute-start.12 = (bf16[6,1,5120]{2,0,1:T(8,128)(2,1)S(1)}, bf16[6,1,5120]{2,0,1:T(8,128)(2,1)S(1)}, u32[]{:S(2)}, u32[]{:S(2)}) collective-permute-start(bf16[6,1,5120]{2,0,1:T(8,128)(2,1)S(1)} %copy.333), channel_id=1, source_target_pairs={{0,1},{2,3},{4,5},{6,7},{8,9},{10,11},{12,13},{14,15},{16,17},{18,... | collective-permute-start | bytes 184328 | tf_op jit(solution)/shard_map/ppermute | solution.py:16
  443.1 4.9 copy-start.44
  443.4 5.5 collective-permute-start.6
  444.7 4.4 collective-permute-start.5
  481.2 2.1 copy-start.11
  481.2 2.1 copy-start.47
  481.2 2.1 copy-start.49
  481.2 2.1 copy-start.51
  481.2 3.4 copy-start.67
  481.3 45.4 %copy-start.69 = (f32[4]{0:T(128)S(1)}, f32[4]{0:T(128)}, u32[]{:S(2)}) copy-start(f32[4]{0:T(128)} %copy-done.68) | copy-start | bytes 52
  533.7 2.8 copy-start.5
  549.8 150.9 %all-reduce.13.cloned.1.call-start = ((), (), s32[]{:S(2)}) async-start(), calls=%async_computation | async-start | bytes 3538944 | tf_op jit(solution)/shard_map/psum | solution.py:189
  550.3 2.5 copy-start.40
  700.7 2.3 copy-start.30
  (22 other events, 30.3 us)
Sparse Core Ops, SparseCore 0:
  550.0 20.5 all-reduce.14
  580.2 120.4 all-reduce.12
